TPU v7x, 32 devices: a whole 2x2x4 slice. The times are simulated.
32 devices in a mesh: row: 8 (over z, core), col: 4 (over y, x).
Axes of the slice: x: 2, y: 2, z: 4, core: 2. Of those that a mesh axis runs over, the one named last changes fastest.
Arguments:
- context: bfloat16 [128, 16384], P('row', 'col'), may hold values from -6 to 6
- out_weight: bfloat16 [16384, 16384], P('col', 'row'), may hold values from -0.046875 to 0.046875
- residual: bfloat16 [128, 16384], P('col', 'row'), may hold values from -80 to 80
- teacher_gain: float32 [16384], replicated, may hold values from 0.5 to 1.5
- student_hidden: bfloat16 [128, 4096], P(('row', 'col')), may hold values from -6 to 6
- student_gain: float32 [4096], replicated, may hold values from 0.5 to 1.5
- projector: bfloat16 [4096, 16384], P(None, ('row', 'col')), may hold values from -0.09375 to 0.09375
Outputs:
- grad_proj: float32 [4096, 16384], P(None, ('row', 'col'))
- grad_gain: float32 [4096], replicated
- loss: float32 [], replicated
All inputs are finite; a program needn't handle non-finite values.
Results may differ from a plain program's by a relative error of at most 0.0065.
Values may be sent and summed in bfloat16 or wider, within the bound.
A program may use at most 64 MiB of HBM per device.

v0:
```python
import jax
import jax.numpy as jnp
from jax import lax
from jax.sharding import PartitionSpec as P

D_T = 16384
norm_eps = 1e-05


def normalize(hidden):
    widened = hidden.astype(jnp.float32)
    return widened * lax.rsqrt(jnp.mean(widened * widened, axis=1, keepdims=True) + norm_eps)


def per_device(
    context, out_weight, residual, teacher_gain, student_hidden, student_gain, projector
):
    row_index = lax.axis_index("row")
    context_all = lax.all_gather(context, "row", axis=0, tiled=True)
    out_block = out_weight.shape[1]
    summed = lax.psum_scatter(
        jnp.dot(context_all, out_weight, preferred_element_type=jnp.float32),
        "col",
        scatter_dimension=0,
        tiled=True,
    )
    summed = summed + residual.astype(jnp.float32)
    squares = lax.psum(jnp.sum(summed * summed, axis=1), "row")
    gain_block = lax.dynamic_slice_in_dim(teacher_gain, row_index * out_block, out_block)
    final_rows = (summed * lax.rsqrt(squares / D_T + norm_eps)[:, None] * gain_block).astype(
        jnp.bfloat16
    )
    target = lax.all_to_all(final_rows, "col", split_axis=1, concat_axis=0, tiled=True)
    hidden_all = lax.all_gather(student_hidden, ("row", "col"), axis=0, tiled=True)
    normed_all = normalize(hidden_all)
    student_all = (normed_all * student_gain).astype(jnp.bfloat16)
    predicted = jnp.dot(student_all, projector, preferred_element_type=jnp.float32)
    difference = predicted - target.astype(jnp.float32)
    loss_part = jnp.sum(difference * difference)
    loss_total = lax.psum(loss_part, ("row", "col"))
    error_term = (difference * (1.0 / 64.0)).astype(jnp.bfloat16)
    grad_proj = lax.dot_general(
        student_all, error_term, (((0,), (0,)), ((), ())), preferred_element_type=jnp.float32
    )
    grad_normed = lax.dot_general(
        error_term, projector, (((1,), (1,)), ((), ())), preferred_element_type=jnp.float32
    )
    gain_part = jnp.sum(grad_normed * normed_all, axis=0)
    grad_gain = lax.psum(gain_part, ("row", "col"))
    tokens_all = predicted.shape[0]
    loss = loss_total / (tokens_all * D_T)
    return (grad_proj, grad_gain, loss)


def solution(mesh):
    placed = (
        P("row", "col"),
        P("col", "row"),
        P("col", "row"),
        P(),
        P(("row", "col"), None),
        P(),
        P(None, ("row", "col")),
    )
    return jax.shard_map(
        per_device,
        mesh=mesh,
        in_specs=placed,
        out_specs=(P(None, ("row", "col")), P(), P()),
        check_vma=False,
    )
```

profile of v0, /device:TPU:12, one launch (start us, length us, event | category | flops | bytes accessed | tf_op | source)
XLA Modules:
  0.0 205.2 jit_solution(2190091404144003150)
XLA Ops:
  7.2 0.0 all-gather.4.cloned.1.call-start
  7.2 0.7 all-gather.4.cloned.1.call-update
  7.9 0.0 all-gather.6.cloned.1.call-start
  7.9 0.7 all-gather.6.cloned.1.call-update
  8.6 0.0 reduce-scatter.2.cloned.1.call-start
  8.7 24.4 %all-gather.4.cloned.1.call-done = bf16[128,4096]{1,0:T(8,128)(2,1)} async-done(((bf16[16,4096]{1,0:T(8,128)(2,1)}), bf16[128,4096]{1,0:T(8,128)(2,1)}) %all-gather.4.cloned.1.call-update) | async-done | bytes 1048592 | tf_op jit(solution)/shard_map/all_gather | solution.py:19
  33.1 9.4 %fusion.4 = f32[128,2048]{1,0:T(8,128)} fusion(bf16[128,4096]{1,0:T(8,128)(2,1)} %all-gather.4.cloned.1.call-done, bf16[4096,2048]{1,0:T(8,128)(2,1)} %param.8), kind=kOutput, calls=%fused_computation.16 | convolution fusion | flops 2147483648 | bytes 18874368 | tf_op jit(solution)/shard_map/dot_general | solution.py:22
  42.5 0.0 reduce-scatter.2.cloned.1.call-update
  42.5 0.0 copy-start.1
  42.5 0.0 dynamic-slice-start
  42.5 46.0 %all-gather.6.cloned.1.call-done = bf16[32,4,4096]{2,1,0:T(4,128)(2,1)} async-done(((bf16[1,4,4096]{2,1,0:T(4,128)(2,1)}), bf16[32,4,4096]{2,1,0:T(4,128)(2,1)}) %all-gather.6.cloned.1.call-update) | async-done | bytes 1048592 | tf_op jit(solution)/shard_map/all_gather | solution.py:34
  88.5 1.3 reshape.25
  89.8 0.0 copy-start.2
  89.8 0.2 multiply_reduce_fusion
  90.0 29.6 %reduce-scatter.2.cloned.1.call-done = f32[32,2048]{1,0:T(8,128)} async-done(((f32[128,2048]{1,0:T(8,128)}), f32[32,2048]{1,0:T(8,128)}) %reduce-scatter.2.cloned.1.call-update) | async-done | bytes 262160 | tf_op jit(solution)/shard_map/reduce_scatter | solution.py:21
  119.7 0.0 copy-done.1
  119.7 1.1 multiply_reduce_fusion.2
  120.8 12.7 %psum.21 = f32[32]{0:T(128)S(1)} all-reduce(f32[32]{0:T(128)S(1)} %multiply_reduce_fusion.2), channel_id=1, replica_groups=mesh['row'=8,'col'=4] {'row'}, use_global_device_ids=true, to_apply=%region_3.0 | all-reduce | flops 32 | bytes 256 | tf_op jit(solution)/shard_map/psum | solution.py:28
  133.4 0.0 dynamic-slice-done
  133.4 1.0 multiply_convert_fusion.2
  134.5 0.7 copy.14
  135.2 3.9 %all-to-all-start = ((bf16[32,4,512]{2,0,1:T(8,128)(2,1)}), bf16[32,4,512]{2,0,1:T(8,128)(2,1)S(1)}, u32[]{:S(2)}, u32[]{:S(2)}) async-start(bf16[32,4,512]{2,0,1:T(8,128)(2,1)} %bitcast.11), calls=%async_computation.1 | async-start | bytes 262144 | tf_op jit(solution)/shard_map/all_to_all | solution.py:33
  139.0 3.9 %all-to-all-done = bf16[32,4,512]{2,0,1:T(8,128)(2,1)S(1)} async-done(((bf16[32,4,512]{2,0,1:T(8,128)(2,1)}), bf16[32,4,512]{2,0,1:T(8,128)(2,1)S(1)}, u32[]{:S(2)}, u32[]{:S(2)}) %all-to-all-start) | async-done | bytes 131104 | tf_op jit(solution)/shard_map/all_to_all | solution.py:33
  143.0 0.0 copy-done.2
  143.0 0.0 copy-start
  143.0 3.7 %multiply_reduce_fusion.1 = (f32[]{:T(128)}, f32[128,512]{1,0:T(8,128)S(1)}) fusion(f32[128,512]{1,0:T(8,128)S(1)} %bitcast.12, bf16[4096,512]{1,0:T(8,128)(2,1)} %param.13, f32[128,4096]{1,0:T(8,128)S(1)} %reshape.25, f32[4096]{0:T(1024)S(1)} %copy-done.2, f32[128]{0:T(128)S(1)} %add_rsqrt_fusion.1), kind=kOutput, calls=%fused_computation.5 | convolution fusion | flops 538640384 | bytes 6832644 | tf_op jit(solution)/shard_map/dot_general | solution.py:37
  146.7 0.0 copy-done
  146.7 1.5 fusion
  148.2 4.8 %fusion.1 = f32[4096,512]{1,0:T(8,128)} fusion(f32[128,512]{1,0:T(8,128)S(1)} %get-tuple-element.6, f32[128,4096]{1,0:T(8,128)S(1)} %reshape.25, f32[4096]{0:T(1024)S(1)} %copy-done.2, f32[128]{0:T(128)S(1)} %add_rsqrt_fusion.1), kind=kOutput, calls=%fused_computation.11 | convolution fusion | flops 538574848 | bytes 10764800 | tf_op jit(solution)/shard_map/dot_general | solution.py:42
  153.0 43.9 %all-reduce = (f32[4096]{0:T(1024)}, f32[]{:T(128)}) all-reduce(f32[4096]{0:T(1024)S(1)} %fusion, f32[]{:T(128)} %get-tuple-element.5), channel_id=1, replica_groups=mesh['row'=8,'col'=4] {'row','col'}, use_global_device_ids=true, to_apply=%region_5.0 | all-reduce | flops 4097 | bytes 32776 | tf_op jit(solution)/shard_map/psum | solution.py:49
  (3 shorter events, 0.0 us)
Async XLA Ops:
  7.2 25.9 %all-gather.4.cloned.1.call-start = ((), (), s32[]{:S(2)}) async-start(), calls=%async_computation.2 | async-start | bytes 1179648 | tf_op jit(solution)/shard_map/all_gather | solution.py:19
  7.9 80.6 %all-gather.6.cloned.1.call-start = ((), (), s32[]{:S(2)}) async-start(), calls=%async_computation.4 | async-start | bytes 1081344 | tf_op jit(solution)/shard_map/all_gather | solution.py:34
  8.6 111.0 %reduce-scatter.2.cloned.1.call-start = ((), (), s32[]{:S(2)}) async-start(), calls=%async_computation.3 | async-start | bytes 1310720 | tf_op jit(solution)/shard_map/reduce_scatter | solution.py:21
  42.5 77.2 %copy-start.1 = (bf16[32,2048]{1,0:T(8,128)(2,1)S(1)}, bf16[32,2048]{1,0:T(8,128)(2,1)}, u32[]{:S(2)}) copy-start(bf16[32,2048]{1,0:T(8,128)(2,1)} %param.9) | copy-start | bytes 393220
  42.5 90.9 %dynamic-slice-start = ((f32[16384]{0:T(1024)}, s32[]{:T(128)}), f32[2048]{0:T(1024)S(1)}, s32[]{:S(2)}) async-start(f32[16384]{0:T(1024)} %param.10, s32[]{:T(128)} %select_n.3), calls=%async_computation.5 | async-start | bytes 16896 | tf_op jit(solution)/shard_map/dynamic_slice | solution.py:29
  89.8 53.2 %copy-start.2 = (f32[4096]{0:T(1024)S(1)}, f32[4096]{0:T(1024)}, u32[]{:S(2)}) copy-start(f32[4096]{0:T(1024)} %param.12) | copy-start | bytes 49156
  135.2 7.8 %all-to-all-start = ((bf16[32,4,512]{2,0,1:T(8,128)(2,1)}), bf16[32,4,512]{2,0,1:T(8,128)(2,1)S(1)}, u32[]{:S(2)}, u32[]{:S(2)}) async-start(bf16[32,4,512]{2,0,1:T(8,128)(2,1)} %bitcast.11), calls=%async_computation.1 | async-start | bytes 262144 | tf_op jit(solution)/shard_map/all_to_all | solution.py:33
  143.0 3.8 %copy-start = (bf16[4096,512]{1,0:T(8,128)(2,1)S(1)}, bf16[4096,512]{1,0:T(8,128)(2,1)}, u32[]{:S(2)}) copy-start(bf16[4096,512]{1,0:T(8,128)(2,1)} %param.13) | copy-start | bytes 12582916
Sparse Core Ops, SparseCore 0:
  9.6 23.4 all-gather.3
  36.1 52.4 all-gather.5
  92.0 27.6 reduce-scatter.1
where the time goes:
time: 206 us; the launch traced here: 205 us
  waiting for transfers between devices  105 us (51%)
  blocking collectives  56.6 us (27%)
  matrix products  19.4 us (9%)
  between operations  15.6 us (8%)
  starting transfers between devices  3.99 us (2%)
  other arithmetic  2.4 us (1%)
    all_gather x1, waiting for transfers between devices, per_device(): lax.all_gather(student_hidden, ('row', 'col'), axis=0, tiled=True)  46 us
    psum x1, blocking collectives, per_device(): grad_gain = lax.psum(gain_part, ('row', 'col'))  43.9 us
    reduce_scatter x1, waiting for transfers between devices, per_device(): lax.psum_scatter(jnp.dot(context_all, out_weight, preferred_element_type=...  29.6 us
    all_gather x1, waiting for transfers between devices, per_device(): context_all = lax.all_gather(context, 'row', axis=0, tiled=True)  24.4 us
    psum x1, blocking collectives, per_device(): squares = lax.psum(jnp.sum(summed * summed, axis=1), 'row')  12.7 us
    dot_general x1, matrix products, per_device(): jnp.dot(context_all, out_weight, preferred_element_type=jnp.float32)  9.41 us
    dot_general x1, matrix products, per_device(): lax.dot_general(student_all, error_term, (((0,), (0,)), ((), ())), prefer...  4.77 us
  transfers between devices with their start and end apart: 4, of which 4 were waited for; matrix products, arithmetic and copies ran while one was open for 5% of the time, Pallas kernels for 0%

commit v1 on v0

--- a/solution.py
+++ b/solution.py
@@ -16,7 +16,12 @@
     context, out_weight, residual, teacher_gain, student_hidden, student_gain, projector
 ):
     row_index = lax.axis_index("row")
-    context_all = lax.all_gather(context, "row", axis=0, tiled=True)
+    ring = [context]
+    for hop in range(7):
+        ring.append(lax.ppermute(ring[-1], "row", [(dev, (dev + 1) % 8) for dev in range(8)]))
+    context_all = jnp.roll(
+        jnp.concatenate(ring[::-1], axis=0), (lax.axis_index("row") + 1) * ring[0].shape[0], axis=0
+    )
     out_block = out_weight.shape[1]
     summed = lax.psum_scatter(
         jnp.dot(context_all, out_weight, preferred_element_type=jnp.float32),

time: 206 us -> 189 us (0.917)
  waiting for transfers between devices: 105 us -> 86.1 us
    ppermute x0 -> x7, waiting for transfers between devices: none -> 35.1 us  [per_device(): lax.ppermute(ring[-1], 'row', [(dev, (dev + 1) % 8) for dev in range(8)])]
    reduce_scatter x1, waiting for transfers between devices: 29.6 us -> 0.02 us  [per_device(): lax.psum_scatter(jnp.dot(context_all, out_weight, preferred_element_type=...]
    all_gather x1 -> x0, waiting for transfers between devices: 24.4 us -> none  [per_device(): context_all = lax.all_gather(context, 'row', axis=0, tiled=True)]
  transfers between devices with their start and end apart: 4 -> 10, of which waited for: 4 -> 9; matrix products, arithmetic and copies ran while one was open for 5% -> 6% of each run, Pallas kernels for 0% -> 0%
where the time goes in v1:
time: 189 us
  waiting for transfers between devices  86.1 us (46%)
  blocking collectives  56.8 us (30%)
  matrix products  19.1 us (10%)
  between operations  17.5 us (9%)
  starting transfers between devices  4 us (2%)
  local copies, waits for them, and re-layouts  3.06 us (2%)
  other arithmetic  2.4 us (1%)
    all_gather x1, waiting for transfers between devices, per_device(): lax.all_gather(student_hidden, ('row', 'col'), axis=0, tiled=True)  47.1 us
    psum x1, blocking collectives, per_device(): grad_gain = lax.psum(gain_part, ('row', 'col'))  43.9 us
    ppermute x7, waiting for transfers between devices, per_device(): lax.ppermute(ring[-1], 'row', [(dev, (dev + 1) % 8) for dev in range(8)])  35.1 us
    psum x1, blocking collectives, per_device(): squares = lax.psum(jnp.sum(summed * summed, axis=1), 'row')  12.9 us
    dot_general x1, matrix products, per_device(): jnp.dot(context_all, out_weight, preferred_element_type=jnp.float32)  9.1 us
    dot_general x1, matrix products, per_device(): lax.dot_general(student_all, error_term, (((0,), (0,)), ((), ())), prefer...  4.77 us
    all_to_all x1, waiting for transfers between devices, per_device(): lax.all_to_all(final_rows, 'col', split_axis=1, concat_axis=0, tiled=True)  3.91 us
    all_to_all x1, starting transfers between devices, per_device(): lax.all_to_all(final_rows, 'col', split_axis=1, concat_axis=0, tiled=True)  3.85 us
  transfers between devices with their start and end apart: 10, of which 9 were waited for; matrix products, arithmetic and copies ran while one was open for 6% of the time, Pallas kernels for 0%

profile of v1, /device:TPU:12, one launch (start us, length us, event | category | flops | bytes accessed | tf_op | source)
XLA Modules:
  0.0 189.0 jit_solution(12437921234076817069)
XLA Ops:
  8.0 0.0 copy-start.2
  8.0 0.0 all-gather.3.cloned.1.call-start
  8.1 0.1 collective-permute-start
  8.1 4.6 %collective-permute-done = bf16[16,4096]{1,0:T(8,128)(2,1)S(1)} collective-permute-done((bf16[16,4096]{1,0:T(8,128)(2,1)}, bf16[16,4096]{1,0:T(8,128)(2,1)S(1)}, u32[]{:S(2)}, u32[]{:S(2)}) %collective-permute-start) | collective-permute-done | bytes 131104 | tf_op jit(solution)/shard_map/ppermute | solution.py:21
  12.7 0.0 collective-permute-start.1
  12.7 4.4 %collective-permute-done.1 = bf16[16,4096]{1,0:T(8,128)(2,1)S(1)} collective-permute-done((bf16[16,4096]{1,0:T(8,128)(2,1)S(1)}, bf16[16,4096]{1,0:T(8,128)(2,1)S(1)}, u32[]{:S(2)}, u32[]{:S(2)}) %collective-permute-start.1) | collective-permute-done | bytes 131104 | tf_op jit(solution)/shard_map/ppermute | solution.py:21
  17.1 0.0 collective-permute-start.2
  17.1 4.4 %collective-permute-done.2 = bf16[16,4096]{1,0:T(8,128)(2,1)S(1)} collective-permute-done((bf16[16,4096]{1,0:T(8,128)(2,1)S(1)}, bf16[16,4096]{1,0:T(8,128)(2,1)S(1)}, u32[]{:S(2)}, u32[]{:S(2)}) %collective-permute-start.2) | collective-permute-done | bytes 131104 | tf_op jit(solution)/shard_map/ppermute | solution.py:21
  21.5 0.0 collective-permute-start.3
  21.5 4.4 %collective-permute-done.3 = bf16[16,4096]{1,0:T(8,128)(2,1)S(1)} collective-permute-done((bf16[16,4096]{1,0:T(8,128)(2,1)S(1)}, bf16[16,4096]{1,0:T(8,128)(2,1)S(1)}, u32[]{:S(2)}, u32[]{:S(2)}) %collective-permute-start.3) | collective-permute-done | bytes 131104 | tf_op jit(solution)/shard_map/ppermute | solution.py:21
  25.9 0.0 collective-permute-start.4
  25.9 5.1 %collective-permute-done.4 = bf16[16,4096]{1,0:T(8,128)(2,1)S(1)} collective-permute-done((bf16[16,4096]{1,0:T(8,128)(2,1)S(1)}, bf16[16,4096]{1,0:T(8,128)(2,1)S(1)}, u32[]{:S(2)}, u32[]{:S(2)}) %collective-permute-start.4) | collective-permute-done | bytes 131104 | tf_op jit(solution)/shard_map/ppermute | solution.py:21
  30.9 0.0 collective-permute-start.5
  31.0 6.2 %collective-permute-done.5 = bf16[16,4096]{1,0:T(8,128)(2,1)S(1)} collective-permute-done((bf16[16,4096]{1,0:T(8,128)(2,1)S(1)}, bf16[16,4096]{1,0:T(8,128)(2,1)S(1)}, u32[]{:S(2)}, u32[]{:S(2)}) %collective-permute-start.5) | collective-permute-done | bytes 131104 | tf_op jit(solution)/shard_map/ppermute | solution.py:21
  37.1 0.0 collective-permute-start.6
  37.1 0.0 all-gather.3.cloned.1.call-update
  37.2 0.0 reduce-scatter.2.cloned.1.call-start
  37.2 6.1 %collective-permute-done.6 = bf16[16,4096]{1,0:T(8,128)(2,1)S(1)} collective-permute-done((bf16[16,4096]{1,0:T(8,128)(2,1)S(1)}, bf16[16,4096]{1,0:T(8,128)(2,1)S(1)}, u32[]{:S(2)}, u32[]{:S(2)}) %collective-permute-start.6) | collective-permute-done | bytes 131104 | tf_op jit(solution)/shard_map/ppermute | solution.py:21
  43.5 0.9 constant_dynamic-update-slice_fusion.8
  44.5 0.0 copy-done.2
  44.5 9.1 %fusion.1 = f32[128,2048]{1,0:T(8,128)} fusion(bf16[4096,2048]{1,0:T(8,128)(2,1)} %param.8, bf16[256,4096]{1,0:T(8,128)(2,1)S(1)} %constant_dynamic-update-slice_fusion, s32[]{:T(128)S(6)} %select_n.17), kind=kOutput, calls=%fused_computation.5 | convolution fusion | flops 2147483648 | bytes 18874372 | tf_op jit(solution)/shard_map/dot_general | solution.py:27
  53.6 0.0 reduce-scatter.2.cloned.1.call-update
  53.7 0.0 copy-start.1
  53.7 0.0 dynamic-slice-start
  53.7 47.1 %all-gather.3.cloned.1.call-done = bf16[32,4,4096]{2,1,0:T(4,128)(2,1)} async-done(((bf16[1,4,4096]{2,1,0:T(4,128)(2,1)}), bf16[32,4,4096]{2,1,0:T(4,128)(2,1)}) %all-gather.3.cloned.1.call-update) | async-done | bytes 1048592 | tf_op jit(solution)/shard_map/all_gather | solution.py:39
  100.7 1.3 reshape.25
  102.0 0.0 copy-start.3
  102.0 0.2 multiply_reduce_fusion
  102.3 0.0 reduce-scatter.2.cloned.1.call-done
  102.3 0.0 copy-done.1
  102.3 1.1 multiply_reduce_fusion.2
  103.4 12.9 %psum.21 = f32[32]{0:T(128)S(1)} all-reduce(f32[32]{0:T(128)S(1)} %multiply_reduce_fusion.2), channel_id=1, replica_groups=mesh['row'=8,'col'=4] {'row'}, use_global_device_ids=true, to_apply=%region_3.4 | all-reduce | flops 32 | bytes 256 | tf_op jit(solution)/shard_map/psum | solution.py:33
  116.4 0.0 dynamic-slice-done
  116.4 1.0 multiply_convert_fusion.2
  117.4 0.7 copy.14
  118.1 3.8 %all-to-all-start = ((bf16[32,4,512]{2,0,1:T(8,128)(2,1)}), bf16[32,4,512]{2,0,1:T(8,128)(2,1)S(1)}, u32[]{:S(2)}, u32[]{:S(2)}) async-start(bf16[32,4,512]{2,0,1:T(8,128)(2,1)} %bitcast.10), calls=%async_computation.1 | async-start | bytes 262144 | tf_op jit(solution)/shard_map/all_to_all | solution.py:38
  121.9 3.9 %all-to-all-done = bf16[32,4,512]{2,0,1:T(8,128)(2,1)S(1)} async-done(((bf16[32,4,512]{2,0,1:T(8,128)(2,1)}), bf16[32,4,512]{2,0,1:T(8,128)(2,1)S(1)}, u32[]{:S(2)}, u32[]{:S(2)}) %all-to-all-start) | async-done | bytes 131104 | tf_op jit(solution)/shard_map/all_to_all | solution.py:38
  125.9 0.0 copy-done.3
  125.9 0.0 copy-start
  125.9 3.7 %multiply_reduce_fusion.1 = (f32[]{:T(128)}, f32[128,512]{1,0:T(8,128)S(1)}) fusion(f32[128,512]{1,0:T(8,128)S(1)} %bitcast.11, bf16[4096,512]{1,0:T(8,128)(2,1)} %param.13, f32[128,4096]{1,0:T(8,128)S(1)} %reshape.25, f32[4096]{0:T(1024)S(1)} %copy-done.3, f32[128]{0:T(128)S(1)} %add_rsqrt_fusion.1), kind=kOutput, calls=%fused_computation.7 | convolution fusion | flops 538640384 | bytes 6832644 | tf_op jit(solution)/shard_map/dot_general | solution.py:42
  129.6 0.0 copy-done
  129.6 1.5 fusion
  131.1 4.8 %fusion.3 = f32[4096,512]{1,0:T(8,128)} fusion(f32[128,512]{1,0:T(8,128)S(1)} %get-tuple-element.6, f32[128,4096]{1,0:T(8,128)S(1)} %reshape.25, f32[4096]{0:T(1024)S(1)} %copy-done.3, f32[128]{0:T(128)S(1)} %add_rsqrt_fusion.1), kind=kOutput, calls=%fused_computation.13 | convolution fusion | flops 538574848 | bytes 10764800 | tf_op jit(solution)/shard_map/dot_general | solution.py:47
  135.9 43.9 %all-reduce = (f32[4096]{0:T(1024)}, f32[]{:T(128)}) all-reduce(f32[4096]{0:T(1024)S(1)} %fusion, f32[]{:T(128)} %get-tuple-element.5), channel_id=1, replica_groups=mesh['row'=8,'col'=4] {'row','col'}, use_global_device_ids=true, to_apply=%region_5.6 | all-reduce | flops 4097 | bytes 32776 | tf_op jit(solution)/shard_map/psum | solution.py:54
  (18 shorter events, 0.2 us)
Async XLA Ops:
  8.0 36.5 %copy-start.2 = (bf16[16,4096]{1,0:T(8,128)(2,1)S(1)}, bf16[16,4096]{1,0:T(8,128)(2,1)}, u32[]{:S(2)}) copy-start(bf16[16,4096]{1,0:T(8,128)(2,1)} %param.7) | copy-start | bytes 393220
  8.0 92.7 %all-gather.3.cloned.1.call-start = ((), (), s32[]{:S(2)}) async-start(), calls=%async_computation.3 | async-start | bytes 1081344 | tf_op jit(solution)/shard_map/all_gather | solution.py:39
  8.1 4.7 %collective-permute-start = (bf16[16,4096]{1,0:T(8,128)(2,1)}, bf16[16,4096]{1,0:T(8,128)(2,1)S(1)}, u32[]{:S(2)}, u32[]{:S(2)}) collective-permute-start(bf16[16,4096]{1,0:T(8,128)(2,1)} %param.7), channel_id=1, source_target_pairs={{0,4},{4,8},{8,12},{12,16},{16,20},{20,24},{24,28},{28,0},{1,5},{5... | collective-permute-start | bytes 393224 | tf_op jit(solution)/shard_map/ppermute | solution.py:21
  12.7 4.4 %collective-permute-start.1 = (bf16[16,4096]{1,0:T(8,128)(2,1)S(1)}, bf16[16,4096]{1,0:T(8,128)(2,1)S(1)}, u32[]{:S(2)}, u32[]{:S(2)}) collective-permute-start(bf16[16,4096]{1,0:T(8,128)(2,1)S(1)} %collective-permute-done), channel_id=1, source_target_pairs={{0,4},{4,8},{8,12},{12,16},{16,20},{20,24},{24,28},{28,0},{1,5},{5... | collective-permute-start | bytes 393224 | tf_op jit(solution)/shard_map/ppermute | solution.py:21
  17.1 4.4 %collective-permute-start.2 = (bf16[16,4096]{1,0:T(8,128)(2,1)S(1)}, bf16[16,4096]{1,0:T(8,128)(2,1)S(1)}, u32[]{:S(2)}, u32[]{:S(2)}) collective-permute-start(bf16[16,4096]{1,0:T(8,128)(2,1)S(1)} %collective-permute-done.1), channel_id=1, source_target_pairs={{0,4},{4,8},{8,12},{12,16},{16,20},{20,24},{24,28},{28,0},{1,5},{5... | collective-permute-start | bytes 393224 | tf_op jit(solution)/shard_map/ppermute | solution.py:21
  21.5 4.4 %collective-permute-start.3 = (bf16[16,4096]{1,0:T(8,128)(2,1)S(1)}, bf16[16,4096]{1,0:T(8,128)(2,1)S(1)}, u32[]{:S(2)}, u32[]{:S(2)}) collective-permute-start(bf16[16,4096]{1,0:T(8,128)(2,1)S(1)} %collective-permute-done.2), channel_id=1, source_target_pairs={{0,4},{4,8},{8,12},{12,16},{16,20},{20,24},{24,28},{28,0},{1,5},{5... | collective-permute-start | bytes 393224 | tf_op jit(solution)/shard_map/ppermute | solution.py:21
  25.9 5.1 %collective-permute-start.4 = (bf16[16,4096]{1,0:T(8,128)(2,1)S(1)}, bf16[16,4096]{1,0:T(8,128)(2,1)S(1)}, u32[]{:S(2)}, u32[]{:S(2)}) collective-permute-start(bf16[16,4096]{1,0:T(8,128)(2,1)S(1)} %collective-permute-done.3), channel_id=1, source_target_pairs={{0,4},{4,8},{8,12},{12,16},{16,20},{20,24},{24,28},{28,0},{1,5},{5... | collective-permute-start | bytes 393224 | tf_op jit(solution)/shard_map/ppermute | solution.py:21
  30.9 6.2 %collective-permute-start.5 = (bf16[16,4096]{1,0:T(8,128)(2,1)S(1)}, bf16[16,4096]{1,0:T(8,128)(2,1)S(1)}, u32[]{:S(2)}, u32[]{:S(2)}) collective-permute-start(bf16[16,4096]{1,0:T(8,128)(2,1)S(1)} %collective-permute-done.4), channel_id=1, source_target_pairs={{0,4},{4,8},{8,12},{12,16},{16,20},{20,24},{24,28},{28,0},{1,5},{5... | collective-permute-start | bytes 393224 | tf_op jit(solution)/shard_map/ppermute | solution.py:21
  37.1 6.2 %collective-permute-start.6 = (bf16[16,4096]{1,0:T(8,128)(2,1)S(1)}, bf16[16,4096]{1,0:T(8,128)(2,1)S(1)}, u32[]{:S(2)}, u32[]{:S(2)}) collective-permute-start(bf16[16,4096]{1,0:T(8,128)(2,1)S(1)} %collective-permute-done.5), channel_id=1, source_target_pairs={{0,4},{4,8},{8,12},{12,16},{16,20},{20,24},{24,28},{28,0},{1,5},{5... | collective-permute-start | bytes 393224 | tf_op jit(solution)/shard_map/ppermute | solution.py:21
  37.2 65.1 %reduce-scatter.2.cloned.1.call-start = ((), (), s32[]{:S(2)}) async-start(), calls=%async_computation.2 | async-start | bytes 1310720 | tf_op jit(solution)/shard_map/reduce_scatter | solution.py:26
  53.7 48.6 %copy-start.1 = (bf16[32,2048]{1,0:T(8,128)(2,1)S(1)}, bf16[32,2048]{1,0:T(8,128)(2,1)}, u32[]{:S(2)}) copy-start(bf16[32,2048]{1,0:T(8,128)(2,1)} %param.9) | copy-start | bytes 393220
  53.7 62.7 %dynamic-slice-start = ((f32[16384]{0:T(1024)}, s32[]{:T(128)}), f32[2048]{0:T(1024)S(1)}, s32[]{:S(2)}) async-start(f32[16384]{0:T(1024)} %param.10, s32[]{:T(128)} %select_n.18), calls=%async_computation.4 | async-start | bytes 16896 | tf_op jit(solution)/shard_map/dynamic_slice | solution.py:34
  102.0 23.8 %copy-start.3 = (f32[4096]{0:T(1024)S(1)}, f32[4096]{0:T(1024)}, u32[]{:S(2)}) copy-start(f32[4096]{0:T(1024)} %param.12) | copy-start | bytes 49156
  118.1 7.8 %all-to-all-start = ((bf16[32,4,512]{2,0,1:T(8,128)(2,1)}), bf16[32,4,512]{2,0,1:T(8,128)(2,1)S(1)}, u32[]{:S(2)}, u32[]{:S(2)}) async-start(bf16[32,4,512]{2,0,1:T(8,128)(2,1)} %bitcast.10), calls=%async_computation.1 | async-start | bytes 262144 | tf_op jit(solution)/shard_map/all_to_all | solution.py:38
  125.9 3.8 %copy-start = (bf16[4096,512]{1,0:T(8,128)(2,1)S(1)}, bf16[4096,512]{1,0:T(8,128)(2,1)}, u32[]{:S(2)}) copy-start(bf16[4096,512]{1,0:T(8,128)(2,1)} %param.13) | copy-start | bytes 12582916
Sparse Core Ops, SparseCore 0:
  37.3 63.4 all-gather.2
Sparse Core Ops, SparseCore 1:
  53.7 34.9 reduce-scatter.1
